TPU v7x, 256 devices: a whole 4x4x8 slice. The times are simulated.
256 devices in a mesh: grp: 8 (over z), blk: 32 (over y, x, core).
Axes of the slice: x: 4, y: 4, z: 8, core: 2. Of those that a mesh axis runs over, the one named last changes fastest.
Arguments:
- embeddings: bfloat16 [8, 2048, 1024], P('grp', 'blk'), may hold values from -72 to 72
- cluster_ids: int32 [8, 2048], P('grp', 'blk'), may hold values from 0 to 63, never falling along the last dimension, each value on 1 to 128 neighbouring positions
- block_list: int32 [8, 256, 2], P('grp', 'blk'), may hold values from 0 to 31, as said below
- block_counts: int32 [8, 32], P('grp', 'blk'), may hold values from 1 to 8, as said below
- pair_targets: float32 [8, 256, 4096], P('grp', 'blk'), may hold values from -6 to 6
- w_left: bfloat16 [1024, 512], replicated, may hold values from -0.125 to 0.125
- w_right: bfloat16 [1024, 512], replicated, may hold values from -0.125 to 0.125
- hidden_bias: float32 [512], replicated, may hold values from -3 to 3
- w_middle: bfloat16 [512, 128], replicated, may hold values from -0.25 to 0.25
- w_final: float32 [128], replicated, may hold values from -0.5 to 0.5
Outputs:
- grad_embeddings: float32 [8, 2048, 1024], P('grp', 'blk')
- grad_left: float32 [1024, 512], replicated
- grad_right: float32 [1024, 512], replicated
- grad_bias: float32 [512], replicated
- grad_middle: float32 [512, 128], replicated
- grad_final: float32 [128], replicated
Inputs may be any that keep to these rules, and one draw needn't show every extreme that they name: `block_list`: entries are panels of the device's own group; the column panel lies within one of the row panel. `block_counts`: slots of a device at and beyond its count are unused; in every group one device has exactly 8.
All inputs are finite; a program needn't handle non-finite values.
Results may differ from a plain program's by a relative error of at most 0.012.
Values may be sent and summed in bfloat16 or wider, within the bound.
No kernel may reach another device: no remote copies, remote signals or barrier semaphores. Data moves between devices by JAX's collectives and lax.ppermute only.
A program may use at most 128 MiB of HBM per device.

v0:
```python
import math
import jax
import jax.numpy as jnp
from jax import lax
from jax.sharding import PartitionSpec as P

PANEL = 64
B_DEV = 8


def silu_slope(value):
    sigmoid_value = jax.nn.sigmoid(value)
    return sigmoid_value * (1.0 + value * (1.0 - sigmoid_value))


def pair_block(
    left_rows,
    right_rows,
    left_ids,
    right_ids,
    row_start,
    col_start,
    pair_target,
    hidden_bias,
    w_middle,
    w_final,
):
    panel_rows = left_rows.shape[0]
    hidden_width = left_rows.shape[1]
    pre_hidden = (
        left_rows.astype(jnp.float32)[:, None, :]
        + right_rows.astype(jnp.float32)[None, :, :]
        + hidden_bias
    )
    hidden = (
        jax.nn.silu(pre_hidden).astype(jnp.bfloat16).reshape(panel_rows * panel_rows, hidden_width)
    )
    pre_upper = jnp.dot(hidden, w_middle, preferred_element_type=jnp.float32)
    upper_act = jax.nn.silu(pre_upper)
    predicted = jnp.sum(upper_act * w_final, axis=1)
    left_pos = row_start + jnp.arange(panel_rows, dtype=jnp.int32)
    right_pos = col_start + jnp.arange(panel_rows, dtype=jnp.int32)
    same_cluster = (left_ids[:, None] == right_ids[None, :]) & (
        left_pos[:, None] != right_pos[None, :]
    )
    residual = jnp.where(same_cluster.reshape(-1), predicted - pair_target, 0.0)
    pair_slope = 16.0 * residual
    grad_final = jnp.sum(upper_act * pair_slope[:, None], axis=0)
    grad_second = (pair_slope[:, None] * w_final[None, :] * silu_slope(pre_upper)).astype(
        jnp.bfloat16
    )
    grad_middle = lax.dot_general(
        hidden, grad_second, (((0,), (0,)), ((), ())), preferred_element_type=jnp.float32
    )
    grad_hidden = lax.dot_general(
        grad_second, w_middle, (((1,), (1,)), ((), ())), preferred_element_type=jnp.float32
    )
    grad_first = grad_hidden.reshape(panel_rows, panel_rows, hidden_width) * silu_slope(pre_hidden)
    return (
        jnp.sum(grad_first, axis=1),
        jnp.sum(grad_first, axis=0),
        jnp.sum(grad_first, axis=(0, 1)),
        grad_middle,
        grad_final,
    )


def local(
    embeddings,
    cluster_ids,
    block_list,
    block_counts,
    pair_targets,
    w_left,
    w_right,
    hidden_bias,
    w_middle,
    w_final,
):
    local_emb = embeddings[0]
    whole_emb, group_ids = (
        lax.all_gather(embeddings, "blk", axis=1, tiled=True),
        lax.all_gather(cluster_ids, "blk", axis=1, tiled=True),
    )
    whole_emb = whole_emb[0]

    def fetch_panels(row_start, col_start):
        row_emb = lax.dynamic_slice_in_dim(whole_emb, row_start, PANEL, 0)
        col_emb = lax.dynamic_slice_in_dim(whole_emb, col_start, PANEL, 0)
        return (
            jnp.dot(row_emb, w_left, preferred_element_type=jnp.float32).astype(jnp.bfloat16),
            jnp.dot(col_emb, w_right, preferred_element_type=jnp.float32).astype(jnp.bfloat16),
        )

    group_ids = group_ids[0]
    local_blocks = block_list[0]
    local_targets = pair_targets[0]
    molecules = group_ids.shape[0]
    hidden_width = w_left.shape[1]

    def slot_step(slot, carry):
        part_left, part_right, sum_bias, sum_middle, sum_final = carry
        entry = lax.dynamic_index_in_dim(local_blocks, slot, 0, keepdims=False)
        row_start = entry[0] * PANEL
        col_start = entry[1] * PANEL
        pair_target = lax.dynamic_index_in_dim(local_targets, slot, 0, keepdims=False)
        left_rows, right_rows = fetch_panels(row_start, col_start)
        grad_rows, grad_cols, grad_bias, grad_middle, grad_final = pair_block(
            left_rows,
            right_rows,
            lax.dynamic_slice_in_dim(group_ids, row_start, PANEL, 0),
            lax.dynamic_slice_in_dim(group_ids, col_start, PANEL, 0),
            row_start,
            col_start,
            pair_target,
            hidden_bias,
            w_middle,
            w_final,
        )
        current = lax.dynamic_slice_in_dim(part_left, row_start, PANEL, 0)
        part_left = lax.dynamic_update_slice_in_dim(part_left, current + grad_rows, row_start, 0)
        current = lax.dynamic_slice_in_dim(part_right, col_start, PANEL, 0)
        part_right = lax.dynamic_update_slice_in_dim(part_right, current + grad_cols, col_start, 0)
        return (
            part_left,
            part_right,
            sum_bias + grad_bias,
            sum_middle + grad_middle,
            sum_final + grad_final,
        )

    empty = jnp.zeros((molecules, hidden_width), jnp.float32)
    start_state = (
        empty,
        empty,
        jnp.zeros((hidden_width,), jnp.float32),
        jnp.zeros(w_middle.shape, jnp.float32),
        jnp.zeros(w_final.shape, jnp.float32),
    )
    part_left, part_right, sum_bias, sum_middle, sum_final = lax.fori_loop(
        0, block_counts[0, 0], slot_step, start_state
    )
    rounded_left = part_left.astype(jnp.bfloat16)
    rounded_right = part_right.astype(jnp.bfloat16)
    own_left, own_right = (
        lax.psum_scatter(
            rounded_left.astype(jnp.float32).astype(jnp.bfloat16),
            "blk",
            scatter_dimension=0,
            tiled=True,
        ).astype(jnp.float32),
        lax.psum_scatter(
            rounded_right.astype(jnp.float32).astype(jnp.bfloat16),
            "blk",
            scatter_dimension=0,
            tiled=True,
        ).astype(jnp.float32),
    )
    left_grad = own_left.astype(jnp.bfloat16)
    right_grad = own_right.astype(jnp.bfloat16)
    grad_local = jnp.dot(left_grad, w_left.T, preferred_element_type=jnp.float32) + jnp.dot(
        right_grad, w_right.T, preferred_element_type=jnp.float32
    )
    weight_left = lax.dot_general(
        local_emb, left_grad, (((0,), (0,)), ((), ())), preferred_element_type=jnp.float32
    )
    weight_right = lax.dot_general(
        local_emb, right_grad, (((0,), (0,)), ((), ())), preferred_element_type=jnp.float32
    )
    summed = lax.psum((weight_left, weight_right, sum_bias, sum_middle, sum_final), ("grp", "blk"))
    devices = lax.axis_size("grp") * lax.axis_size("blk")
    scale = 1.0 / math.sqrt(devices * B_DEV * PANEL)
    return (
        grad_local[None],
        summed[0] * scale,
        summed[1] * scale,
        summed[2] * scale,
        summed[3] * scale,
        summed[4] * scale,
    )


def solution(mesh):
    return jax.shard_map(
        local,
        mesh=mesh,
        in_specs=(
            P("grp", "blk", None),
            P("grp", "blk"),
            P("grp", "blk", None),
            P("grp", "blk"),
            P("grp", "blk", None),
            P(),
            P(),
            P(),
            P(),
            P(),
        ),
        out_specs=(P("grp", "blk", None), P(), P(), P(), P(), P()),
        check_vma=False,
    )
```

profile of v0, /device:TPU:2, one launch (start us, length us, event | category | flops | bytes accessed | tf_op | source)
XLA Modules:
  0.0 784.3 jit_solution(16809696372307641489)
XLA Ops:
  7.2 0.0 all-gather.2.cloned.1.call-start
  7.2 0.7 all-gather.2.cloned.1.call-update
  7.9 0.0 reduce-scatter.5.cloned.1.call-start
  7.9 1.3 dynamic-slice
  9.9 0.8 bitcast_dynamic-update-slice_fusion
  10.7 15.9 %all-reduce = s32[2048]{0:T(1024)S(1)} all-reduce(s32[2048]{0:T(1024)S(1)} %bitcast_dynamic-update-slice_fusion), channel_id=1, replica_groups=mesh['grp'=8,'blk'=32] {'blk'}, use_global_device_ids=true, to_apply=%add | all-reduce | flops 2048 | bytes 16384 | tf_op jit(solution)/shard_map/squeeze | solution.py:95
  26.5 37.7 %all-gather.2.cloned.1.call-done = bf16[1,2048,1024]{2,1,0:T(8,128)(2,1)} async-done(((bf16[1,64,1024]{2,1,0:T(8,128)(2,1)}), bf16[1,2048,1024]{2,1,0:T(8,128)(2,1)}) %all-gather.2.cloned.1.call-update) | async-done | bytes 4194320 | tf_op jit(solution)/shard_map/all_gather | solution.py:82
  64.3 2.5 broadcast_in_dim.14
  66.7 2.5 broadcast_in_dim.14.clone
  69.2 0.7 broadcast_in_dim.16
  70.0 60.5 %while.18 = (s32[]{:T(128)}, f32[2048,512]{1,0:T(8,128)}, f32[2048,512]{1,0:T(8,128)}, f32[512]{0:T(512)S(1)}, f32[512,128]{1,0:T(8,128)}, /*index=5*/f32[128]{0...) while((s32[]{:T(128)}, f32[2048,512]{1,0:T(8,128)}, ...), condition=%wide.region_6.7_spmd, body=%wide.region_0.6_spmd.sunk | while | flops 1822642304 | bytes 153014800 | solution.py:140
  70.6 0.1 constant_dynamic-slice_fusion.4
  70.7 0.5 fusion.48
  71.9 1.2 fusion.50
  73.7 1.6 fusion.49
  75.3 1.1 broadcast_add_fusion.2
  76.5 3.4 multiply_convert_fusion.7
  79.9 1.3 multiply_reduce_fusion.6
  81.2 0.6 copy-done.2
  81.9 0.1 fusion.51
  81.9 0.1 compare_and_fusion.2
  82.0 0.1 and.15
  82.1 0.9 constant_dynamic-slice_fusion.5
  83.1 5.0 convolution_add_fusion.3
  88.1 5.3 multiply_reduce_fusion.7
  93.4 3.9 fusion.52
  97.3 1.7 add_dynamic-update-slice_fusion.3
  99.1 0.7 multiply_reduce_fusion.8
  100.5 0.1 constant_dynamic-slice_fusion.4
  100.5 0.5 fusion.48
  101.7 1.2 fusion.50
  103.6 1.6 fusion.49
  105.2 1.1 broadcast_add_fusion.2
  106.3 3.4 multiply_convert_fusion.7
  109.7 1.3 multiply_reduce_fusion.6
  111.1 0.6 copy-done.2
  111.7 0.1 fusion.51
  111.8 0.1 compare_and_fusion.2
  111.9 0.1 and.15
  112.0 0.9 constant_dynamic-slice_fusion.5
  112.9 5.0 convolution_add_fusion.3
  118.0 5.3 multiply_reduce_fusion.7
  123.2 3.9 fusion.52
  127.2 1.7 add_dynamic-update-slice_fusion.3
  128.9 0.7 multiply_reduce_fusion.8
  130.5 3.8 convert_element_type.34
  134.2 0.0 reduce-scatter.5.cloned.1.call-update
  134.3 0.0 reduce-scatter.3.cloned.1.call-start
  134.3 3.8 convert_element_type.33
  138.2 0.0 all-reduce.5.cloned.1.call-start
  138.2 261.0 %reduce-scatter.5.cloned.1.call-done = bf16[64,512]{1,0:T(8,128)(2,1)} async-done(((bf16[2048,512]{1,0:T(8,128)(2,1)}), bf16[64,512]{1,0:T(8,128)(2,1)}) %reduce-scatter.5.cloned.1.call-update) | async-done | bytes 65552 | tf_op jit(solution)/shard_map/reduce_scatter | solution.py:152
  399.2 2.6 convolution_bitcast_fusion
  401.8 87.8 %reduce-scatter.3.cloned.1.call-done = bf16[64,512]{1,0:T(8,128)(2,1)} async-done(((bf16[2048,512]{1,0:T(8,128)(2,1)}), bf16[64,512]{1,0:T(8,128)(2,1)}) %reduce-scatter.3.cloned.1.call-update) | async-done | bytes 65552 | tf_op jit(solution)/shard_map/reduce_scatter | solution.py:146
  489.6 2.7 convolution_bitcast_fusion.1
  492.3 73.9 %all-reduce.1 = (f32[512]{0:T(512)S(1)}, f32[128]{0:T(128)S(1)}) all-reduce(f32[512]{0:T(512)S(1)} %get-tuple-element.95, f32[128]{0:T(128)S(1)} %get-tuple-element.97), channel_id=1, replica_groups=mesh['grp'=8,'blk'=32] {'grp','blk'}, use_global_device_ids=true, to_apply=%region_11.12 | all-reduce | flops 640 | bytes 5120 | tf_op jit(solution)/shard_map/psum | solution.py:170
  566.2 0.5 broadcast_multiply_fusion.4
  566.7 0.6 broadcast_multiply_fusion.3
  567.3 0.4 fusion.14
  567.7 2.4 fusion.8
  570.1 198.0 %all-reduce.5.cloned.1.call-done = (f32[1024,512]{0,1:T(8,128)}, f32[1024,512]{0,1:T(8,128)}, f32[512,128]{1,0:T(8,128)}) async-done(((f32[1024,512]{0,1:T(8,128)}, f32[1024,512]{0,1:T(8,128)}, f32[512,128]{1,0:T(8,128)}), (f32[1024,512]{0,1:T(8,128)}, f32[1024,512]{0,1:T(8,128)}, f32[512,128]{1,0:T(8,128)})) %all-reduce.5.cloned.1.call-update) | async-done | bytes 4456464 | tf_op jit(solution)/shard_map/psum | solution.py:170
  768.1 4.2 broadcast_multiply_fusion
  772.3 2.9 copy.16
  775.2 1.8 copy.17
  777.0 0.7 broadcast_multiply_fusion.2
  (49 shorter events, 0.2 us)
Async XLA Ops:
  7.2 57.1 %all-gather.2.cloned.1.call-start = ((), (), s32[]{:S(2)}) async-start(), calls=%async_computation.2 | async-start | bytes 4325376 | tf_op jit(solution)/shard_map/all_gather | solution.py:82
  7.9 391.3 %reduce-scatter.5.cloned.1.call-start = ((), (), s32[]{:S(2)}) async-start(), calls=%async_computation.4 | async-start | bytes 2162688 | tf_op jit(solution)/shard_map/reduce_scatter | solution.py:152
  64.2 5.7 copy-start.3
  64.3 5.7 copy-start.8
  64.3 5.7 copy-start.9
  64.3 5.7 copy-start.12
  76.5 3.4 copy-start
  76.5 3.4 copy-start.10
  79.9 2.0 copy-start.2
  83.1 5.1 copy-start.1
  83.1 5.1 copy-start.11
  106.3 3.4 copy-start
  106.3 3.4 copy-start.10
  109.7 2.0 copy-start.2
  112.9 5.1 copy-start.1
  112.9 5.1 copy-start.11
  134.3 355.3 %reduce-scatter.3.cloned.1.call-start = ((), (), s32[]{:S(2)}) async-start(), calls=%async_computation.3 | async-start | bytes 2162688 | tf_op jit(solution)/shard_map/reduce_scatter | solution.py:146
  134.3 264.9 %copy-start.4 = (bf16[1,64,1024]{2,1,0:T(8,128)(2,1)S(1)}, bf16[1,64,1024]{2,1,0:T(8,128)(2,1)}, u32[]{:S(2)}) copy-start(bf16[1,64,1024]{2,1,0:T(8,128)(2,1)} %param.12) | copy-start | bytes 393220
  138.2 629.9 %all-reduce.5.cloned.1.call-start = ((), (), s32[]{:S(2)}) async-start(), calls=%async_computation.5 | async-start | bytes 8912896 | tf_op jit(solution)/shard_map/psum | solution.py:170
  401.8 165.9 %copy-start.5 = (bf16[64,512]{1,0:T(8,128)(2,1)S(1)}, bf16[64,512]{1,0:T(8,128)(2,1)}, u32[]{:S(2)}) copy-start(bf16[64,512]{1,0:T(8,128)(2,1)} %reduce-scatter.5.cloned.1.call-done) | copy-start | bytes 196612
  489.6 77.7 %copy-start.7 = (bf16[64,512]{1,0:T(8,128)(2,1)S(1)}, bf16[64,512]{1,0:T(8,128)(2,1)}, u32[]{:S(2)}) copy-start(bf16[64,512]{1,0:T(8,128)(2,1)} %reduce-scatter.3.cloned.1.call-done) | copy-start | bytes 196612
  772.3 4.7 copy-start.6
Sparse Core Ops, SparseCore 0:
  10.5 53.6 all-gather.1
  134.4 264.7 reduce-scatter.4
  403.6 85.9 reduce-scatter.2
  495.8 272.2 all-reduce.4
where the time goes:
time: 786 us; the launch traced here: 784 us
  waiting for transfers between devices  585 us (74%)
  blocking collectives  89.8 us (11%)
  matrix products  37 us (5%)
  other arithmetic  35.6 us (5%)
  local copies, waits for them, and re-layouts  17.1 us (2%)
  between operations  14.5 us (2%)
    reduce_scatter x1, waiting for transfers between devices, local(): lax.psum_scatter(rounded_right.astype(jnp.float32).astype(jnp.bfloat16),...  261 us
    psum x1, waiting for transfers between devices, local(): lax.psum((weight_left, weight_right, sum_bias, sum_middle, sum_final), ('...  198 us
    reduce_scatter x1, waiting for transfers between devices, local(): lax.psum_scatter(rounded_left.astype(jnp.float32).astype(jnp.bfloat16), '...  87.8 us
    psum x1, blocking collectives, local(): lax.psum((weight_left, weight_right, sum_bias, sum_middle, sum_final), ('...  73.9 us
    all_gather x1, waiting for transfers between devices, local(): lax.all_gather(embeddings, 'blk', axis=1, tiled=True)  37.7 us
    squeeze x1, blocking collectives, local(): group_ids = group_ids[0]  15.9 us
  transfers between devices with their start and end apart: 4, of which 4 were waited for; matrix products, arithmetic and copies ran while one was open for 2% of the time, Pallas kernels for 0%

commit v1 on v0

--- a/solution.py
+++ b/solution.py
@@ -167,7 +167,8 @@
     weight_right = lax.dot_general(
         local_emb, right_grad, (((0,), (0,)), ((), ())), preferred_element_type=jnp.float32
     )
-    summed = lax.psum((weight_left, weight_right, sum_bias, sum_middle, sum_final), ("grp", "blk"))
+    one_axis = lax.psum((weight_left, weight_right, sum_bias, sum_middle, sum_final), "grp")
+    summed = lax.psum(one_axis, "blk")
     devices = lax.axis_size("grp") * lax.axis_size("blk")
     scale = 1.0 / math.sqrt(devices * B_DEV * PANEL)
     return (

time: 786 us -> 749 us (0.953)
  waiting for transfers between devices: 585 us -> 548 us
    psum x1 -> x2, waiting for transfers between devices: 198 us -> 160 us  [the longest x1 114 us: local(): lax.psum((weight_left, weight_right, sum_bias, sum_middle, sum_final), 'g...]
    psum x1 -> x2, blocking collectives: 73.9 us -> 73.9 us  [the longest x1 58.4 us: local(): summed = lax.psum(one_axis, 'blk')]
  transfers between devices with their start and end apart: 4 -> 5, of which waited for: 4 -> 5; matrix products, arithmetic and copies ran while one was open for 2% -> 2% of each run, Pallas kernels for 0% -> 0%
where the time goes in v1:
time: 749 us; the launch traced here: 747 us
  waiting for transfers between devices  548 us (73%)
  blocking collectives  89.8 us (12%)
  matrix products  36.9 us (5%)
  other arithmetic  35.6 us (5%)
  local copies, waits for them, and re-layouts  17.1 us (2%)
  between operations  14.5 us (2%)
    reduce_scatter x1, waiting for transfers between devices, local(): lax.psum_scatter(rounded_right.astype(jnp.float32).astype(jnp.bfloat16),...  261 us
    psum x1, waiting for transfers between devices, local(): lax.psum((weight_left, weight_right, sum_bias, sum_middle, sum_final), 'g...  114 us
    reduce_scatter x1, waiting for transfers between devices, local(): lax.psum_scatter(rounded_left.astype(jnp.float32).astype(jnp.bfloat16), '...  87.8 us
    psum x1, blocking collectives, local(): summed = lax.psum(one_axis, 'blk')  58.4 us
    psum x1, waiting for transfers between devices, local(): summed = lax.psum(one_axis, 'blk')  46.4 us
    all_gather x1, waiting for transfers between devices, local(): lax.all_gather(embeddings, 'blk', axis=1, tiled=True)  37.7 us
    squeeze x1, blocking collectives, local(): group_ids = group_ids[0]  15.9 us
    psum x1, blocking collectives, local(): lax.psum((weight_left, weight_right, sum_bias, sum_middle, sum_final), 'g...  15.5 us
  transfers between devices with their start and end apart: 5, of which 5 were waited for; matrix products, arithmetic and copies ran while one was open for 2% of the time, Pallas kernels for 0%

profile of v1, /device:TPU:2, one launch (start us, length us, event | category | flops | bytes accessed | tf_op | source)
XLA Modules:
  0.0 746.8 jit_solution(6427941696506572078)
XLA Ops:
  7.2 0.7 all-gather.2.cloned.1.call-update
  7.9 1.3 dynamic-slice
  9.9 0.8 bitcast_dynamic-update-slice_fusion
  10.7 15.9 %all-reduce = s32[2048]{0:T(1024)S(1)} all-reduce(s32[2048]{0:T(1024)S(1)} %bitcast_dynamic-update-slice_fusion), channel_id=1, replica_groups=mesh['grp'=8,'blk'=32] {'blk'}, use_global_device_ids=true, to_apply=%add | all-reduce | flops 2048 | bytes 16384 | tf_op jit(solution)/shard_map/squeeze | solution.py:95
  26.5 37.7 %all-gather.2.cloned.1.call-done = bf16[1,2048,1024]{2,1,0:T(8,128)(2,1)} async-done(((bf16[1,64,1024]{2,1,0:T(8,128)(2,1)}), bf16[1,2048,1024]{2,1,0:T(8,128)(2,1)}) %all-gather.2.cloned.1.call-update) | async-done | bytes 4194320 | tf_op jit(solution)/shard_map/all_gather | solution.py:82
  64.3 2.5 broadcast_in_dim.14
  66.7 2.5 broadcast_in_dim.14.clone
  69.2 0.7 broadcast_in_dim.16
  70.0 60.5 %while.18 = (s32[]{:T(128)}, f32[2048,512]{1,0:T(8,128)}, f32[2048,512]{1,0:T(8,128)}, f32[512]{0:T(512)S(1)}, f32[512,128]{1,0:T(8,128)}, /*index=5*/f32[128]{0...) while((s32[]{:T(128)}, f32[2048,512]{1,0:T(8,128)}, ...), condition=%wide.region_6.7_spmd, body=%wide.region_0.6_spmd.sunk | while | flops 1822642304 | bytes 153014800 | solution.py:140
  70.6 0.1 constant_dynamic-slice_fusion.4
  70.7 0.5 fusion.48
  71.9 1.2 fusion.50
  73.7 1.6 fusion.49
  75.3 1.1 broadcast_add_fusion.2
  76.5 3.4 multiply_convert_fusion.7
  79.9 1.3 multiply_reduce_fusion.6
  81.2 0.6 copy-done.2
  81.9 0.1 fusion.51
  81.9 0.1 compare_and_fusion.2
  82.0 0.1 and.15
  82.1 0.9 constant_dynamic-slice_fusion.5
  83.1 5.0 convolution_add_fusion.3
  88.1 5.3 multiply_reduce_fusion.7
  93.4 3.9 fusion.52
  97.3 1.7 add_dynamic-update-slice_fusion.3
  99.1 0.7 multiply_reduce_fusion.8
  100.5 0.1 constant_dynamic-slice_fusion.4
  100.5 0.5 fusion.48
  101.7 1.2 fusion.50
  103.6 1.6 fusion.49
  105.2 1.1 broadcast_add_fusion.2
  106.3 3.4 multiply_convert_fusion.7
  109.7 1.3 multiply_reduce_fusion.6
  111.1 0.6 copy-done.2
  111.7 0.1 fusion.51
  111.8 0.1 compare_and_fusion.2
  111.9 0.1 and.15
  112.0 0.9 constant_dynamic-slice_fusion.5
  112.9 5.0 convolution_add_fusion.3
  118.0 5.3 multiply_reduce_fusion.7
  123.2 3.9 fusion.52
  127.2 1.7 add_dynamic-update-slice_fusion.3
  128.9 0.7 multiply_reduce_fusion.8
  130.5 3.8 convert_element_type.34
  134.3 0.0 reduce-scatter.3.cloned.1.call-start
  134.3 3.8 convert_element_type.33
  138.2 0.0 all-reduce.10.cloned.1.call-start
  138.2 261.0 %reduce-scatter.5.cloned.1.call-done = bf16[64,512]{1,0:T(8,128)(2,1)} async-done(((bf16[2048,512]{1,0:T(8,128)(2,1)}), bf16[64,512]{1,0:T(8,128)(2,1)}) %reduce-scatter.5.cloned.1.call-update) | async-done | bytes 65552 | tf_op jit(solution)/shard_map/reduce_scatter | solution.py:152
  399.2 2.6 convolution_bitcast_fusion
  401.8 87.8 %reduce-scatter.3.cloned.1.call-done = bf16[64,512]{1,0:T(8,128)(2,1)} async-done(((bf16[2048,512]{1,0:T(8,128)(2,1)}), bf16[64,512]{1,0:T(8,128)(2,1)}) %reduce-scatter.3.cloned.1.call-update) | async-done | bytes 65552 | tf_op jit(solution)/shard_map/reduce_scatter | solution.py:146
  489.6 2.6 convolution_bitcast_fusion.1
  492.2 0.0 all-reduce.8.cloned.1.call-start
  492.3 114.0 %all-reduce.10.cloned.1.call-done = (f32[1024,512]{0,1:T(8,128)}, f32[1024,512]{0,1:T(8,128)}, f32[512,128]{1,0:T(8,128)}) async-done(((f32[1024,512]{0,1:T(8,128)}, f32[1024,512]{0,1:T(8,128)}, f32[512,128]{1,0:T(8,128)}), (f32[1024,512]{0,1:T(8,128)}, f32[1024,512]{0,1:T(8,128)}, f32[512,128]{1,0:T(8,128)})) %all-reduce.10.cloned.1.call-update) | async-done | bytes 4456464 | tf_op jit(solution)/shard_map/psum | solution.py:170
  606.3 15.5 %all-reduce.3 = (f32[512]{0:T(512)S(1)}, f32[128]{0:T(128)S(1)}) all-reduce(f32[512]{0:T(512)S(1)} %get-tuple-element.95, f32[128]{0:T(128)S(1)} %get-tuple-element.97), channel_id=1, replica_groups=mesh['grp'=8,'blk'=32] {'grp'}, use_global_device_ids=true, to_apply=%region_13.14 | all-reduce | flops 640 | bytes 5120 | tf_op jit(solution)/shard_map/psum | solution.py:170
  621.9 58.4 %all-reduce.1 = (f32[512]{0:T(512)S(1)}, f32[128]{0:T(128)S(1)}) all-reduce(f32[512]{0:T(512)S(1)} %get-tuple-element.143, f32[128]{0:T(128)S(1)} %get-tuple-element.144), channel_id=1, replica_groups=mesh['grp'=8,'blk'=32] {'blk'}, use_global_device_ids=true, to_apply=%region_14.15 | all-reduce | flops 640 | bytes 5120 | tf_op jit(solution)/shard_map/psum | solution.py:171
  680.2 0.5 broadcast_multiply_fusion.4
  680.8 0.6 broadcast_multiply_fusion.3
  681.3 0.4 fusion.14
  681.8 2.4 fusion.8
  684.2 46.4 %all-reduce.8.cloned.1.call-done = (f32[1024,512]{0,1:T(8,128)}, f32[1024,512]{0,1:T(8,128)}, f32[512,128]{1,0:T(8,128)}) async-done(((f32[1024,512]{0,1:T(8,128)}, f32[1024,512]{0,1:T(8,128)}, f32[512,128]{1,0:T(8,128)}), (f32[1024,512]{0,1:T(8,128)}, f32[1024,512]{0,1:T(8,128)}, f32[512,128]{1,0:T(8,128)})) %all-reduce.8.cloned.1.call-update) | async-done | bytes 4456464 | tf_op jit(solution)/shard_map/psum | solution.py:171
  730.6 4.2 broadcast_multiply_fusion
  734.8 2.9 copy.16
  737.8 1.8 copy.17
  739.6 0.7 broadcast_multiply_fusion.2
  (53 shorter events, 0.3 us)
Async XLA Ops:
  7.2 57.1 %all-gather.2.cloned.1.call-start = ((), (), s32[]{:S(2)}) async-start(), calls=%async_computation.2 | async-start | bytes 4325376 | tf_op jit(solution)/shard_map/all_gather | solution.py:82
  7.9 391.3 %reduce-scatter.5.cloned.1.call-start = ((), (), s32[]{:S(2)}) async-start(), calls=%async_computation.4 | async-start | bytes 2162688 | tf_op jit(solution)/shard_map/reduce_scatter | solution.py:152
  64.2 5.7 copy-start.3
  64.3 5.7 copy-start.8
  64.3 5.7 copy-start.9
  64.3 5.7 copy-start.12
  76.5 3.4 copy-start
  76.5 3.4 copy-start.10
  79.9 2.0 copy-start.2
  83.1 5.1 copy-start.1
  83.1 5.1 copy-start.11
  106.3 3.4 copy-start
  106.3 3.4 copy-start.10
  109.7 2.0 copy-start.2
  112.9 5.1 copy-start.1
  112.9 5.1 copy-start.11
  134.3 355.3 %reduce-scatter.3.cloned.1.call-start = ((), (), s32[]{:S(2)}) async-start(), calls=%async_computation.3 | async-start | bytes 2162688 | tf_op jit(solution)/shard_map/reduce_scatter | solution.py:146
  134.3 264.9 %copy-start.4 = (bf16[1,64,1024]{2,1,0:T(8,128)(2,1)S(1)}, bf16[1,64,1024]{2,1,0:T(8,128)(2,1)}, u32[]{:S(2)}) copy-start(bf16[1,64,1024]{2,1,0:T(8,128)(2,1)} %param.12) | copy-start | bytes 393220
  138.2 468.2 %all-reduce.10.cloned.1.call-start = ((), (), s32[]{:S(2)}) async-start(), calls=%async_computation.6 | async-start | bytes 8912896 | tf_op jit(solution)/shard_map/psum | solution.py:170
  492.2 189.1 %copy-start.7 = (bf16[64,512]{1,0:T(8,128)(2,1)S(1)}, bf16[64,512]{1,0:T(8,128)(2,1)}, u32[]{:S(2)}) copy-start(bf16[64,512]{1,0:T(8,128)(2,1)} %reduce-scatter.3.cloned.1.call-done) | copy-start | bytes 196612
  492.2 189.6 %copy-start.5 = (bf16[64,512]{1,0:T(8,128)(2,1)S(1)}, bf16[64,512]{1,0:T(8,128)(2,1)}, u32[]{:S(2)}) copy-start(bf16[64,512]{1,0:T(8,128)(2,1)} %reduce-scatter.5.cloned.1.call-done) | copy-start | bytes 196612
  492.2 238.4 %all-reduce.8.cloned.1.call-start = ((), (), s32[]{:S(2)}) async-start(), calls=%async_computation.5 | async-start | bytes 8912896 | tf_op jit(solution)/shard_map/psum | solution.py:171
  734.8 4.7 copy-start.6
Sparse Core Ops, SparseCore 0:
  10.5 53.6 all-gather.1
  134.4 264.7 reduce-scatter.4
  403.6 85.9 reduce-scatter.2
  492.6 113.6 all-reduce.9
  609.9 120.6 all-reduce.7
